TPU v7x, 32 devices: a whole 2x2x4 slice. The times are simulated.
32 devices in a mesh: parts: 2 (over x), rows: 16 (over z, y, core).
Axes of the slice: x: 2, y: 2, z: 4, core: 2. Of those that a mesh axis runs over, the one named last changes fastest.
Arguments:
- rhs: float32 [3, 12288, 256], P(None, 'rows', 'parts'), parts along dimension 2, may hold values from -6 to 6
- diag_inv: float32 [3, 12288, 768], P(None, 'rows'), may hold values from -0.21875 to 0.21875
- tiles: float32 [2, 32, 768, 768], P(None, 'rows'), may hold values from -0.15625 to 0.15625
- dest: int32 [2, 16, 2], P(None, 'rows'), may hold values from 0 to 15, all different within a row; in each aligned block of 16 rows (0 to 15, 16 to 31, ..., all dimensions but the last counted through in order) at most 4 rows name the same one
- obs_weight: float32 [12288], P('rows'), may hold values from -0.108253175 to 0.108253175, as said below
Outputs:
- solution: float32 [3, 12288, 256], P(None, 'rows', 'parts'), parts along dimension 2
- observed: float32 [256], P('parts'), parts along dimension 0
There are 2 independent parts, one for each index of `parts`. A program takes and returns all parts, laid end to end along the dimension named above; an argument that names none is the same for every part. Nothing has to cross between parts.
Inputs may be any that keep to these rules, and one draw needn't show every extreme that they name: `dest`: in each of the two levels, the two entries of a supernode differ, and no supernode of the next level is named more than 4 times. `obs_weight`: finite weights.
All inputs are finite; a program needn't handle non-finite values.
Results may differ from a plain program's by a relative error of at most 0.00029.
Values sent between devices are 32-bit elements; how exact they have to be, the bound alone decides.
No kernel may reach another device: no remote copies, remote signals or barrier semaphores. Data moves between devices by JAX's collectives and lax.ppermute only.
A program may use at most 128 MiB of HBM per device.

v0:
```python
import jax
import jax.numpy as jnp
from jax import lax
from jax.sharding import PartitionSpec as P


def collect_updates(solved_block, tiles_level, pattern_level):
    products = jnp.einsum(
        "kab,bc->kac",
        tiles_level,
        solved_block,
        precision=lax.Precision.HIGHEST,
        preferred_element_type=jnp.float32,
    )
    block_rows = solved_block.shape[0]
    width = products.shape[2]
    count = lax.axis_size("rows")
    sliced = lax.all_to_all(products, "rows", split_axis=1, concat_axis=0, tiled=True)
    owners = jnp.arange(count, dtype=jnp.int32)
    flat_targets = pattern_level.reshape(-1)
    matches = (owners[:, None] == flat_targets[None, :]).astype(jnp.float32)
    partial_value = jnp.einsum("mq,qac->mac", matches, sliced, precision=lax.Precision.HIGHEST)
    returned = lax.all_to_all(partial_value, "rows", split_axis=0, concat_axis=0, tiled=True)
    return returned.reshape(block_rows, width)


def body(rhs, diag_inv, tiles, dest, obs_weight):
    pattern = lax.all_gather(dest, "rows", axis=1, tiled=True)
    current = rhs[0]
    solved_levels = []
    solved_block = current
    for section in range(3):
        solved_block = jnp.dot(
            diag_inv[section],
            current,
            precision=lax.Precision.HIGHEST,
            preferred_element_type=jnp.float32,
        )
        solved_levels.append(solved_block)
        if section < 2:
            current = rhs[section + 1] - collect_updates(
                solved_block, tiles[section], pattern[section]
            )
    partial_sum = jnp.dot(
        obs_weight,
        solved_block,
        precision=lax.Precision.HIGHEST,
        preferred_element_type=jnp.float32,
    )
    observed = lax.psum(partial_sum, "rows")
    return (jnp.stack(solved_levels), observed)


def solution(mesh):
    in_specs = (
        P(None, "rows", "parts"),
        P(None, "rows", None),
        P(None, "rows", None, None),
        P(None, "rows", None),
        P("rows"),
    )
    out_specs = (P(None, "rows", "parts"), P("parts"))
    return jax.shard_map(body, mesh=mesh, in_specs=in_specs, out_specs=out_specs, check_vma=False)
```

profile of v0, /device:TPU:0, one launch (start us, length us, event | category | flops | bytes accessed | tf_op | source)
XLA Modules:
  0.0 156.5 jit_solution(14306570408259959369)
XLA Ops:
  0.6 3.7 %fusion.10 = f32[768,128]{1,0:T(8,128)S(1)} fusion(f32[3,768,768]{2,1,0:T(8,128)} %param.6, f32[3,768,128]{2,1,0:T(8,128)} %param.5), kind=kOutput, calls=%fused_computation.10 | convolution fusion | flops 905969664 | bytes 3145728 | tf_op jit(solution)/shard_map/dot_general | solution.py:33
  4.3 7.4 %fusion.15 = f32[2,768,128]{1,2,0:T(8,128)S(1)} fusion(f32[2,2,768,768]{3,2,1,0:T(8,128)} %param.7, f32[768,128]{1,0:T(8,128)S(1)} %fusion.10), kind=kOutput, calls=%fused_computation.15 | convolution fusion | flops 1811939328 | bytes 5898240 | tf_op jit(solution)/shard_map/kab,bc->kac/dot_general | solution.py:8
  11.7 1.2 copy.23
  12.9 7.5 %all-to-all-start = ((f32[2,768,128]{2,0,1:T(2,128)}), f32[2,768,128]{2,0,1:T(2,128)S(1)}, u32[]{:S(2)}, u32[]{:S(2)}) async-start(f32[2,768,128]{2,0,1:T(2,128)} %copy.23), calls=%async_computation | async-start | bytes 1572864 | tf_op jit(solution)/shard_map/all_to_all | solution.py:18
  20.4 29.2 %all_gather.3 = s32[2,16,2]{2,0,1:T(2,128)S(1)} all-gather(s32[2,1,2]{2,0,1:T(2,128)S(1)} %bitcast.82), channel_id=1, replica_groups=mesh['parts'=2,'rows'=16] {'rows'}, dimensions={1}, use_global_device_ids=true | all-gather | bytes 272 | tf_op jit(solution)/shard_map/all_gather | solution.py:28
  49.8 0.6 copy.25
  50.5 0.4 fusion.29
  50.8 0.1 copy.26
  51.0 16.7 %all_to_all.46 = f32[16,48,128]{2,1,0:T(8,128)S(1)} all-to-all(f32[16,48,128]{2,1,0:T(8,128)S(1)} %copy.26), channel_id=1, replica_groups=mesh['parts'=2,'rows'=16] {'rows'}, dimensions={0} | all-to-all | bytes 786432 | tf_op jit(solution)/shard_map/all_to_all | solution.py:23
  67.8 3.8 %fusion.8 = f32[128,768]{1,0:T(8,128)S(1)} fusion(f32[3,768,768]{2,1,0:T(8,128)} %param.6, f32[1,768,128]{2,1,0:T(8,128)S(1)} %bitcast_subtract_fusion.1), kind=kOutput, calls=%fused_computation.8 | convolution fusion | flops 905969664 | bytes 3145728 | tf_op jit(solution)/shard_map/dot_general | solution.py:33
  71.5 5.0 %fusion.18 = f32[2,768,128]{1,2,0:T(8,128)S(1)} fusion(f32[2,2,768,768]{3,2,1,0:T(8,128)S(1)} %copy-done, f32[128,768]{1,0:T(8,128)S(1)} %fusion.8), kind=kOutput, calls=%fused_computation.16 | convolution fusion | flops 1811939328 | bytes 5898240 | tf_op jit(solution)/shard_map/kab,bc->kac/dot_general | solution.py:8
  76.5 1.2 copy.28
  77.7 3.6 %all-to-all-start.2 = ((f32[2,768,128]{2,0,1:T(2,128)}), f32[2,768,128]{2,0,1:T(2,128)S(1)}, u32[]{:S(2)}, u32[]{:S(2)}) async-start(f32[2,768,128]{2,0,1:T(2,128)} %copy.28), calls=%async_computation.2 | async-start | bytes 1572864 | tf_op jit(solution)/shard_map/all_to_all | solution.py:18
  81.4 18.6 %all-to-all-done.2 = f32[2,768,128]{2,0,1:T(2,128)S(1)} async-done(((f32[2,768,128]{2,0,1:T(2,128)}), f32[2,768,128]{2,0,1:T(2,128)S(1)}, u32[]{:S(2)}, u32[]{:S(2)}) %all-to-all-start.2) | async-done | bytes 786464 | tf_op jit(solution)/shard_map/all_to_all | solution.py:18
  100.0 0.6 copy.30
  100.6 0.4 fusion.32
  101.0 0.9 copy.31
  101.9 5.3 %all-to-all-start.3 = ((f32[16,48,128]{2,1,0:T(8,128)}), f32[16,48,128]{2,1,0:T(8,128)S(1)}, u32[]{:S(2)}, u32[]{:S(2)}) async-start(f32[16,48,128]{2,1,0:T(8,128)} %copy.31), calls=%async_computation.3 | async-start | bytes 786432 | tf_op jit(solution)/shard_map/all_to_all | solution.py:23
  107.3 0.2 copy.27
  107.4 12.0 %all-to-all-done.3 = f32[16,48,128]{2,1,0:T(8,128)S(1)} async-done(((f32[16,48,128]{2,1,0:T(8,128)}), f32[16,48,128]{2,1,0:T(8,128)S(1)}, u32[]{:S(2)}, u32[]{:S(2)}) %all-to-all-start.3) | async-done | bytes 393248 | tf_op jit(solution)/shard_map/all_to_all | solution.py:23
  119.4 3.7 %fusion.6 = f32[128,768]{0,1:T(8,128)S(1)} fusion(f32[3,768,768]{2,1,0:T(8,128)} %param.6, f32[1,768,128]{2,1,0:T(8,128)S(1)} %bitcast_subtract_fusion), kind=kOutput, calls=%fused_computation.6 | convolution fusion | flops 905969664 | bytes 3145728 | tf_op jit(solution)/shard_map/dot_general | solution.py:33
  123.1 0.3 convolution_bitcast_fusion
  123.4 32.0 %psum.7 = f32[128]{0:T(128)} all-reduce(f32[128]{0:T(128)S(1)} %convolution_bitcast_fusion), channel_id=1, replica_groups=mesh['parts'=2,'rows'=16] {'rows'}, use_global_device_ids=true, to_apply=%region_0.0 | all-reduce | flops 128 | bytes 1024 | tf_op jit(solution)/shard_map/psum | solution.py:50
  155.4 1.1 pad_maximum_fusion
  (17 shorter events, 0.4 us)
Async XLA Ops:
  11.7 8.7 %copy-start.3 = (s32[2,1,2]{2,1,0:T(1,128)S(1)}, s32[2,1,2]{2,1,0:T(1,128)}, u32[]{:S(2)}) copy-start(s32[2,1,2]{2,1,0:T(1,128)} %param.8) | copy-start | bytes 52
  12.9 54.8 %copy-start.1 = (f32[3,768,128]{2,1,0:T(8,128)S(1)}, f32[3,768,128]{2,1,0:T(8,128)}, u32[]{:S(2)}) copy-start(f32[3,768,128]{2,1,0:T(8,128)} %param.5) | copy-start | bytes 3538948
  12.9 36.9 %all-to-all-start = ((f32[2,768,128]{2,0,1:T(2,128)}), f32[2,768,128]{2,0,1:T(2,128)S(1)}, u32[]{:S(2)}, u32[]{:S(2)}) async-start(f32[2,768,128]{2,0,1:T(2,128)} %copy.23), calls=%async_computation | async-start | bytes 1572864 | tf_op jit(solution)/shard_map/all_to_all | solution.py:18
  49.8 21.8 %copy-start = (f32[2,2,768,768]{3,2,1,0:T(8,128)S(1)}, f32[2,2,768,768]{3,2,1,0:T(8,128)}, u32[]{:S(2)}) copy-start(f32[2,2,768,768]{3,2,1,0:T(8,128)} %param.7) | copy-start | bytes 28311556
  77.7 22.3 %all-to-all-start.2 = ((f32[2,768,128]{2,0,1:T(2,128)}), f32[2,768,128]{2,0,1:T(2,128)S(1)}, u32[]{:S(2)}, u32[]{:S(2)}) async-start(f32[2,768,128]{2,0,1:T(2,128)} %copy.28), calls=%async_computation.2 | async-start | bytes 1572864 | tf_op jit(solution)/shard_map/all_to_all | solution.py:18
  100.0 7.2 %copy-start.2 = (f32[768]{0:T(1024)S(1)}, f32[768]{0:T(1024)}, u32[]{:S(2)}) copy-start(f32[768]{0:T(1024)} %param.9) | copy-start | bytes 9220
  101.9 17.5 %all-to-all-start.3 = ((f32[16,48,128]{2,1,0:T(8,128)}), f32[16,48,128]{2,1,0:T(8,128)S(1)}, u32[]{:S(2)}, u32[]{:S(2)}) async-start(f32[16,48,128]{2,1,0:T(8,128)} %copy.31), calls=%async_computation.3 | async-start | bytes 786432 | tf_op jit(solution)/shard_map/all_to_all | solution.py:23
where the time goes:
time: 157 us
  blocking collectives  77.9 us (50%)
  waiting for transfers between devices  30.5 us (19%)
  matrix products  24.5 us (16%)
  starting transfers between devices  16.5 us (11%)
  local copies, waits for them, and re-layouts  5.05 us (3%)
    psum x1, blocking collectives, body(): observed = lax.psum(partial_sum, 'rows')  32 us
    all_gather x1, blocking collectives, body(): pattern = lax.all_gather(dest, 'rows', axis=1, tiled=True)  29.2 us
    all_to_all x2, waiting for transfers between devices, collect_updates(): lax.all_to_all(products, 'rows', split_axis=1, concat_axis=0, tiled=True)  18.6 us
    all_to_all x1, blocking collectives, collect_updates(): lax.all_to_all(partial_value, 'rows', split_axis=0, concat_axis=0, tiled=...  16.7 us
    dot_general x2, matrix products, collect_updates(): jnp.einsum('kab,bc->kac', tiles_level, solved_block, precision=lax.Precis...  12.3 us
    all_to_all x1, waiting for transfers between devices, collect_updates(): lax.all_to_all(partial_value, 'rows', split_axis=0, concat_axis=0, tiled=...  12 us
    all_to_all x2, starting transfers between devices, collect_updates(): lax.all_to_all(products, 'rows', split_axis=1, concat_axis=0, tiled=True)  11.2 us
    dot_general x3, matrix products, body(): jnp.dot(diag_inv[section], current, precision=lax.Precision.HIGHEST, pref...  11.1 us
  transfers between devices with their start and end apart: 3, of which 2 were waited for; matrix products, arithmetic and copies ran while one was open for 0% of the time, Pallas kernels for 0%

commit v1 on v0

--- a/solution.py
+++ b/solution.py
@@ -25,7 +25,8 @@
 
 
 def body(rhs, diag_inv, tiles, dest, obs_weight):
-    pattern = lax.all_gather(dest, "rows", axis=1, tiled=True)
+    pieces = lax.all_gather(dest, "rows")
+    pattern = jnp.concatenate(pieces, axis=1)
     current = rhs[0]
     solved_levels = []
     solved_block = current

time: 157 us -> 158 us (level)
  transfers between devices with their start and end apart: 3 -> 3, of which waited for: 2 -> 2; matrix products, arithmetic and copies ran while one was open for 0% -> 1% of each run, Pallas kernels for 0% -> 0%
where the time goes in v1:
time: 158 us; the launch traced here: 157 us
  blocking collectives  77.9 us (49%)
  waiting for transfers between devices  30.3 us (19%)
  matrix products  24.5 us (16%)
  starting transfers between devices  16.5 us (10%)
  local copies, waits for them, and re-layouts  5.68 us (4%)
    psum x1, blocking collectives, body(): observed = lax.psum(partial_sum, 'rows')  32 us
    all_gather x1, blocking collectives, body(): pieces = lax.all_gather(dest, 'rows')  29.2 us
    all_to_all x2, waiting for transfers between devices, collect_updates(): lax.all_to_all(products, 'rows', split_axis=1, concat_axis=0, tiled=True)  18.3 us
    all_to_all x1, blocking collectives, collect_updates(): lax.all_to_all(partial_value, 'rows', split_axis=0, concat_axis=0, tiled=...  16.7 us
    dot_general x2, matrix products, collect_updates(): jnp.einsum('kab,bc->kac', tiles_level, solved_block, precision=lax.Precis...  12.3 us
    all_to_all x1, waiting for transfers between devices, collect_updates(): lax.all_to_all(partial_value, 'rows', split_axis=0, concat_axis=0, tiled=...  12 us
    all_to_all x2, starting transfers between devices, collect_updates(): lax.all_to_all(products, 'rows', split_axis=1, concat_axis=0, tiled=True)  11.2 us
    dot_general x3, matrix products, body(): jnp.dot(diag_inv[section], current, precision=lax.Precision.HIGHEST, pref...  11.1 us
  transfers between devices with their start and end apart: 3, of which 2 were waited for; matrix products, arithmetic and copies ran while one was open for 1% of the time, Pallas kernels for 0%

profile of v1, /device:TPU:0, one launch (start us, length us, event | category | flops | bytes accessed | tf_op | source)
XLA Modules:
  0.0 157.0 jit_solution(13151353748151247654)
XLA Ops:
  0.6 3.7 %fusion.10 = f32[768,128]{1,0:T(8,128)S(1)} fusion(f32[3,768,768]{2,1,0:T(8,128)} %param.6, f32[3,768,128]{2,1,0:T(8,128)} %param.5), kind=kOutput, calls=%fused_computation.10 | convolution fusion | flops 905969664 | bytes 3145728 | tf_op jit(solution)/shard_map/dot_general | solution.py:34
  4.3 7.4 %fusion.15 = f32[2,768,128]{1,2,0:T(8,128)S(1)} fusion(f32[2,2,768,768]{3,2,1,0:T(8,128)} %param.7, f32[768,128]{1,0:T(8,128)S(1)} %fusion.10), kind=kOutput, calls=%fused_computation.15 | convolution fusion | flops 1811939328 | bytes 5898240 | tf_op jit(solution)/shard_map/kab,bc->kac/dot_general | solution.py:8
  11.7 1.2 copy.30
  12.9 7.5 %all-to-all-start = ((f32[2,768,128]{2,0,1:T(2,128)}), f32[2,768,128]{2,0,1:T(2,128)S(1)}, u32[]{:S(2)}, u32[]{:S(2)}) async-start(f32[2,768,128]{2,0,1:T(2,128)} %copy.30), calls=%async_computation | async-start | bytes 1572864 | tf_op jit(solution)/shard_map/all_to_all | solution.py:18
  20.4 29.2 %all-gather = s32[32,1,2]{2,1,0:T(1,128)S(1)} all-gather(s32[2,1,2]{2,1,0:T(1,128)S(1)} %copy-done.3), channel_id=2, replica_groups=mesh['parts'=2,'rows'=16] {'rows'}, dimensions={0}, use_global_device_ids=true | all-gather | bytes 272 | tf_op jit(solution)/shard_map/all_gather | solution.py:28
  49.6 0.2 copy.43
  50.3 0.6 copy.32
  50.9 0.4 fusion.29
  51.4 16.7 %all_to_all.46 = f32[16,48,128]{2,1,0:T(8,128)S(1)} all-to-all(f32[16,48,128]{2,1,0:T(8,128)S(1)} %copy.33), channel_id=1, replica_groups=mesh['parts'=2,'rows'=16] {'rows'}, dimensions={0} | all-to-all | bytes 786432 | tf_op jit(solution)/shard_map/all_to_all | solution.py:23
  68.2 3.8 %fusion.8 = f32[128,768]{1,0:T(8,128)S(1)} fusion(f32[3,768,768]{2,1,0:T(8,128)} %param.6, f32[1,768,128]{2,1,0:T(8,128)S(1)} %bitcast_subtract_fusion.1), kind=kOutput, calls=%fused_computation.8 | convolution fusion | flops 905969664 | bytes 3145728 | tf_op jit(solution)/shard_map/dot_general | solution.py:34
  72.0 5.0 %fusion.18 = f32[2,768,128]{1,2,0:T(8,128)S(1)} fusion(f32[2,2,768,768]{3,2,1,0:T(8,128)S(1)} %copy-done, f32[128,768]{1,0:T(8,128)S(1)} %fusion.8), kind=kOutput, calls=%fused_computation.16 | convolution fusion | flops 1811939328 | bytes 5898240 | tf_op jit(solution)/shard_map/kab,bc->kac/dot_general | solution.py:8
  76.9 1.2 copy.36
  78.1 3.6 %all-to-all-start.2 = ((f32[2,768,128]{2,0,1:T(2,128)}), f32[2,768,128]{2,0,1:T(2,128)S(1)}, u32[]{:S(2)}, u32[]{:S(2)}) async-start(f32[2,768,128]{2,0,1:T(2,128)} %copy.36), calls=%async_computation.2 | async-start | bytes 1572864 | tf_op jit(solution)/shard_map/all_to_all | solution.py:18
  81.7 0.2 copy.35
  82.0 18.3 %all-to-all-done.2 = f32[2,768,128]{2,0,1:T(2,128)S(1)} async-done(((f32[2,768,128]{2,0,1:T(2,128)}), f32[2,768,128]{2,0,1:T(2,128)S(1)}, u32[]{:S(2)}, u32[]{:S(2)}) %all-to-all-start.2) | async-done | bytes 786464 | tf_op jit(solution)/shard_map/all_to_all | solution.py:18
  100.4 0.6 copy.38
  101.1 0.4 fusion.32
  101.5 0.9 copy.39
  102.3 5.3 %all-to-all-start.3 = ((f32[16,48,128]{2,1,0:T(8,128)}), f32[16,48,128]{2,1,0:T(8,128)S(1)}, u32[]{:S(2)}, u32[]{:S(2)}) async-start(f32[16,48,128]{2,1,0:T(8,128)} %copy.39), calls=%async_computation.3 | async-start | bytes 786432 | tf_op jit(solution)/shard_map/all_to_all | solution.py:23
  107.8 12.0 %all-to-all-done.3 = f32[16,48,128]{2,1,0:T(8,128)S(1)} async-done(((f32[16,48,128]{2,1,0:T(8,128)}), f32[16,48,128]{2,1,0:T(8,128)S(1)}, u32[]{:S(2)}, u32[]{:S(2)}) %all-to-all-start.3) | async-done | bytes 393248 | tf_op jit(solution)/shard_map/all_to_all | solution.py:23
  119.9 3.7 %fusion.6 = f32[128,768]{0,1:T(8,128)S(1)} fusion(f32[3,768,768]{2,1,0:T(8,128)} %param.6, f32[1,768,128]{2,1,0:T(8,128)S(1)} %bitcast_subtract_fusion), kind=kOutput, calls=%fused_computation.6 | convolution fusion | flops 905969664 | bytes 3145728 | tf_op jit(solution)/shard_map/dot_general | solution.py:34
  123.5 0.3 convolution_bitcast_fusion
  123.8 32.0 %psum.7 = f32[128]{0:T(128)} all-reduce(f32[128]{0:T(128)S(1)} %convolution_bitcast_fusion), channel_id=1, replica_groups=mesh['parts'=2,'rows'=16] {'rows'}, use_global_device_ids=true, to_apply=%region_0.0 | all-reduce | flops 128 | bytes 1024 | tf_op jit(solution)/shard_map/psum | solution.py:51
  155.9 1.1 pad_maximum_fusion
  (20 shorter events, 1.0 us)
Async XLA Ops:
  11.7 8.7 %copy-start.3 = (s32[2,1,2]{2,1,0:T(1,128)S(1)}, s32[2,1,2]{2,1,0:T(1,128)}, u32[]{:S(2)}) copy-start(s32[2,1,2]{2,1,0:T(1,128)} %param.8) | copy-start | bytes 52
  12.9 55.2 %copy-start.1 = (f32[3,768,128]{2,1,0:T(8,128)S(1)}, f32[3,768,128]{2,1,0:T(8,128)}, u32[]{:S(2)}) copy-start(f32[3,768,128]{2,1,0:T(8,128)} %param.5) | copy-start | bytes 3538948
  12.9 37.3 %all-to-all-start = ((f32[2,768,128]{2,0,1:T(2,128)}), f32[2,768,128]{2,0,1:T(2,128)S(1)}, u32[]{:S(2)}, u32[]{:S(2)}) async-start(f32[2,768,128]{2,0,1:T(2,128)} %copy.30), calls=%async_computation | async-start | bytes 1572864 | tf_op jit(solution)/shard_map/all_to_all | solution.py:18
  50.2 21.7 %copy-start = (f32[2,2,768,768]{3,2,1,0:T(8,128)S(1)}, f32[2,2,768,768]{3,2,1,0:T(8,128)}, u32[]{:S(2)}) copy-start(f32[2,2,768,768]{3,2,1,0:T(8,128)} %param.7) | copy-start | bytes 28311556
  78.1 22.3 %all-to-all-start.2 = ((f32[2,768,128]{2,0,1:T(2,128)}), f32[2,768,128]{2,0,1:T(2,128)S(1)}, u32[]{:S(2)}, u32[]{:S(2)}) async-start(f32[2,768,128]{2,0,1:T(2,128)} %copy.36), calls=%async_computation.2 | async-start | bytes 1572864 | tf_op jit(solution)/shard_map/all_to_all | solution.py:18
  100.4 7.2 %copy-start.2 = (f32[768]{0:T(1024)S(1)}, f32[768]{0:T(1024)}, u32[]{:S(2)}) copy-start(f32[768]{0:T(1024)} %param.9) | copy-start | bytes 9220
  102.3 17.5 %all-to-all-start.3 = ((f32[16,48,128]{2,1,0:T(8,128)}), f32[16,48,128]{2,1,0:T(8,128)S(1)}, u32[]{:S(2)}, u32[]{:S(2)}) async-start(f32[16,48,128]{2,1,0:T(8,128)} %copy.39), calls=%async_computation.3 | async-start | bytes 786432 | tf_op jit(solution)/shard_map/all_to_all | solution.py:23
